TPU v7x, 32 devices: a whole 2x2x4 slice. The times are simulated.
32 devices in a mesh: groups: 2 (over x), fsdp: 8 (over z, y), dp: 2 (over core).
Axes of the slice: x: 2, y: 2, z: 4, core: 2. Of those that a mesh axis runs over, the one named last changes fastest.
Arguments:
- resid: bfloat16 [512, 5120], P(('groups', 'dp'), 'fsdp'), parts along dimension 0, may hold values from -6 to 6
- hidden_act: bfloat16 [512, 6912], P(('groups', 'dp')), parts along dimension 0, may hold values from -11 to 11
- w_down: bfloat16 [6912, 5120], P(None, 'fsdp'), may hold values from -0.078125 to 0.078125
- norm_gain: bfloat16 [5120], P('fsdp'), may hold values from 0.3 to 4, as said below
- head: bfloat16 [5120, 16384], P(None, 'fsdp'), may hold values from -0.25 to 0.25
- data_ids: int32 [512], P(('groups', 'dp')), parts along dimension 0, may hold values from 0 to 16383
- pseudo_ids: int32 [512], P(('groups', 'dp')), parts along dimension 0, may hold values from 0 to 16383
Outputs:
- scores: float32 [512], P(('groups', 'dp')), parts along dimension 0
There are 2 independent parts, one for each index of `groups`. A program takes and returns all parts, laid end to end along the dimension named above; an argument that names none is the same for every part. Nothing has to cross between parts.
Inputs may be any that keep to these rules, and one draw needn't show every extreme that they name: `norm_gain`: positive gains.
All inputs are finite; a program needn't handle non-finite values.
Results may differ from a plain program's by a relative error of at most 0.012.
Values may be sent and summed in bfloat16 or wider, within the bound.
No kernel may reach another device: no remote copies, remote signals or barrier semaphores. Data moves between devices by JAX's collectives and lax.ppermute only.
A program may use at most 192 MiB of HBM per device.

v0:
```python
import jax
import jax.numpy as jnp
from jax import lax
from jax.sharding import PartitionSpec as P

ITERS = 3
cap_value = 30.0
norm_eps = 1e-05
damping = 0.05


def row_total(values):
    return lax.psum(values, "fsdp")


def per_device(resid, hidden_act, w_down, norm_gain, head, data_ids, pseudo_ids):
    tok_rows = hidden_act.shape[0]
    total_rows = tok_rows * lax.axis_size("dp")
    shard_cols = w_down.shape[1]
    width = shard_cols * lax.axis_size("fsdp")
    vocab_cols = head.shape[1]
    vocab_ids = lax.axis_index("fsdp") * vocab_cols + lax.broadcasted_iota(
        jnp.int32, (1, vocab_cols), 1
    )
    gain = norm_gain.astype(jnp.float32)

    def head_logits(normed_shard):
        return jnp.dot(
            lax.all_gather(normed_shard, "fsdp", axis=1, tiled=True),
            head,
            preferred_element_type=jnp.float32,
        )

    def head_project(weighted):
        return (
            lax.psum_scatter(
                lax.dot_general(
                    head, weighted, (((1,), (1,)), ((), ())), preferred_element_type=jnp.float32
                ).astype(jnp.bfloat16),
                "fsdp",
                scatter_dimension=0,
                tiled=True,
            )
            .astype(jnp.float32)
            .T
        )

    z = resid.astype(jnp.float32) + jnp.dot(hidden_act, w_down, preferred_element_type=jnp.float32)
    inv = lax.rsqrt(row_total(jnp.sum(z * z, axis=1, keepdims=True)) / width + norm_eps)
    normed = (z * inv * gain).astype(jnp.bfloat16)
    capped = cap_value * jnp.tanh(head_logits(normed) / cap_value)
    slope = 1.0 - (capped / cap_value) ** 2
    expval = jnp.exp(capped)
    prob = expval / row_total(jnp.sum(expval, axis=1, keepdims=True))

    def norm_back(upstream):
        scaled = gain * head_project((upstream * slope).astype(jnp.bfloat16))
        mixed = row_total(jnp.sum(z * scaled, axis=1, keepdims=True)) / width
        return inv * scaled - z * inv**3 * mixed

    def tangent(full_vector):
        zv = jnp.dot(hidden_act, full_vector, preferred_element_type=jnp.float32)
        inv_t = -(inv**3) * row_total(jnp.sum(z * zv, axis=1, keepdims=True)) / width
        moved = (gain * (zv * inv + z * inv_t)).astype(jnp.bfloat16)
        return slope * head_logits(moved)

    def full_rows(vector):
        return lax.all_gather(vector.astype(jnp.bfloat16), "dp", axis=0, tiled=True)

    def param_sum(dz):
        local = lax.dot_general(
            hidden_act,
            dz.astype(jnp.bfloat16),
            (((0,), (0,)), ((), ())),
            preferred_element_type=jnp.float32,
        )
        return lax.psum_scatter(
            local.astype(jnp.bfloat16), "dp", scatter_dimension=0, tiled=True
        ).astype(jnp.float32)

    def global_dot(values):
        return lax.psum(values, ("fsdp", "dp"))

    pseudo_hot = (pseudo_ids[:, None] == vocab_ids).astype(jnp.float32)
    grad = param_sum(norm_back((prob - pseudo_hot) / total_rows))
    solution = jnp.zeros_like(grad)
    remain = grad
    search = grad
    norm_now = global_dot(jnp.sum(remain * remain))
    for step in range(ITERS):
        change = tangent(full_rows(search))
        inner = row_total(jnp.sum(prob * change, axis=1, keepdims=True))
        image = param_sum(norm_back((prob * change - prob * inner) / total_rows)) + damping * search
        alpha = norm_now / global_dot(jnp.sum(search * image))
        solution = solution + alpha * search
        remain = remain - alpha * image
        if step + 1 < ITERS:
            norm_next = global_dot(jnp.sum(remain * remain))
            search = remain + norm_next / norm_now * search
            norm_now = norm_next
    data_hot = (data_ids[:, None] == vocab_ids).astype(jnp.float32)
    return row_total(jnp.sum((prob - data_hot) * tangent(full_rows(solution)), axis=1))


def solution(mesh):
    placed = (
        P(("groups", "dp"), "fsdp"),
        P(("groups", "dp"), None),
        P(None, "fsdp"),
        P("fsdp"),
        P(None, "fsdp"),
        P(("groups", "dp")),
        P(("groups", "dp")),
    )
    return jax.shard_map(
        per_device, mesh=mesh, in_specs=placed, out_specs=P(("groups", "dp")), check_vma=False
    )
```

profile of v0, /device:TPU:0, one launch (start us, length us, event | category | flops | bytes accessed | tf_op | source)
XLA Modules:
  0.0 1366.7 jit_solution(14872717110527854634)
XLA Ops:
  13.2 23.2 %psum.140 = f32[128,1]{0,1:T(1,128)S(1)} all-reduce(f32[128,1]{0,1:T(1,128)S(1)} %bitcast.129), channel_id=1, replica_groups=mesh['groups'=2,'fsdp'=8,'dp'=2] {'fsdp'}, use_global_device_ids=true, to_apply=%region_1.0 | all-reduce | flops 128 | bytes 1024 | tf_op jit(solution)/shard_map/psum | solution.py:13
  37.2 39.9 %all-gather.10.cloned.1.call-done = bf16[128,5120]{1,0:T(8,128)(2,1)} async-done(((bf16[128,640]{1,0:T(8,128)(2,1)}), bf16[128,5120]{1,0:T(8,128)(2,1)}) %all-gather.10.cloned.1.call-update) | async-done | bytes 1310736 | tf_op jit(solution)/shard_map/all_gather | solution.py:29
  77.1 11.3 fusion.23
  88.4 19.0 %psum.141 = f32[128]{0:T(128)S(1)} all-reduce(f32[128]{0:T(128)S(1)} %get-tuple-element.17), channel_id=1, replica_groups=mesh['groups'=2,'fsdp'=8,'dp'=2] {'fsdp'}, use_global_device_ids=true, to_apply=%region_3.0 | all-reduce | flops 128 | bytes 1024 | tf_op jit(solution)/shard_map/psum | solution.py:13
  107.4 11.5 fusion.11
  120.5 62.6 %reduce-scatter.25.cloned.1.call-done = bf16[640,128]{1,0:T(8,128)(2,1)} async-done(((bf16[5120,128]{1,0:T(8,128)(2,1)}), bf16[640,128]{1,0:T(8,128)(2,1)}) %reduce-scatter.25.cloned.1.call-update) | async-done | bytes 163856
  184.2 19.0 %psum.142 = f32[128,1]{0,1:T(1,128)S(1)} all-reduce(f32[128,1]{0,1:T(1,128)S(1)} %bitcast.130), channel_id=1, replica_groups=mesh['groups'=2,'fsdp'=8,'dp'=2] {'fsdp'}, use_global_device_ids=true, to_apply=%region_6.0 | all-reduce | flops 128 | bytes 1024 | tf_op jit(solution)/shard_map/psum | solution.py:13
  209.3 12.6 copy.22
  222.0 14.1 %reduce-scatter.27.cloned.1.call-done = bf16[3456,640]{1,0:T(8,128)(2,1)} async-done(((bf16[6912,640]{1,0:T(8,128)(2,1)}), bf16[3456,640]{1,0:T(8,128)(2,1)}) %reduce-scatter.27.cloned.1.call-update) | async-done | bytes 4423696
  236.1 7.2 copy.23
  243.5 22.2 %all-gather.12.cloned.1.call-done = bf16[6912,640]{0,1:T(8,128)(2,1)} async-done(((bf16[3456,640]{0,1:T(8,128)(2,1)}), bf16[6912,640]{0,1:T(8,128)(2,1)}) %all-gather.12.cloned.1.call-update) | async-done | bytes 8847376 | tf_op jit(solution)/shard_map/all_gather | solution.py:68
  265.7 6.4 multiply_reduce_fusion.7
  272.1 21.6 %psum.144 = f32[128,1]{0,1:T(1,128)S(1)} all-reduce(f32[128,1]{0,1:T(1,128)S(1)} %bitcast.134), channel_id=1, replica_groups=mesh['groups'=2,'fsdp'=8,'dp'=2] {'fsdp'}, use_global_device_ids=true, to_apply=%region_11.0 | all-reduce | flops 128 | bytes 1024 | tf_op jit(solution)/shard_map/psum | solution.py:13
  294.6 39.9 %all-gather.14.cloned.1.call-done = bf16[128,5120]{1,0:T(8,128)(2,1)} async-done(((bf16[128,640]{1,0:T(8,128)(2,1)}), bf16[128,5120]{1,0:T(8,128)(2,1)}) %all-gather.14.cloned.1.call-update) | async-done | bytes 1310736 | tf_op jit(solution)/shard_map/all_gather | solution.py:29
  334.5 11.5 fusion.82
  346.0 19.0 %psum.145 = f32[128]{0:T(128)S(1)} all-reduce(f32[128]{0:T(128)S(1)} %get-tuple-element.21), channel_id=1, replica_groups=mesh['groups'=2,'fsdp'=8,'dp'=2] {'fsdp'}, use_global_device_ids=true, to_apply=%region_13.0 | all-reduce | flops 128 | bytes 1024 | tf_op jit(solution)/shard_map/psum | solution.py:13
  365.0 11.9 fusion.12
  378.4 62.5 %reduce-scatter.29.cloned.1.call-done = bf16[640,128]{1,0:T(8,128)(2,1)} async-done(((bf16[5120,128]{1,0:T(8,128)(2,1)}), bf16[640,128]{1,0:T(8,128)(2,1)}) %reduce-scatter.29.cloned.1.call-update) | async-done | bytes 163856
  442.1 19.2 %psum.146 = f32[128,1]{0,1:T(1,128)S(1)} all-reduce(f32[128,1]{0,1:T(1,128)S(1)} %bitcast.131), channel_id=1, replica_groups=mesh['groups'=2,'fsdp'=8,'dp'=2] {'fsdp'}, use_global_device_ids=true, to_apply=%region_16.0 | all-reduce | flops 128 | bytes 1024 | tf_op jit(solution)/shard_map/psum | solution.py:13
  467.3 12.6 copy.26
  480.3 13.6 reduce-scatter.31.cloned.1.call-done
  493.9 7.2 copy.27
  506.5 34.5 %all-reduce = (f32[]{:T(128)}, f32[]{:T(128)}) all-reduce(f32[]{:T(128)} %get-tuple-element.6, f32[]{:T(128)} %get-tuple-element.5), channel_id=1, replica_groups=mesh['groups'=2,'fsdp'=8,'dp'=2] {'fsdp','dp'}, use_global_device_ids=true, to_apply=%region_9.0 | all-reduce | flops 2 | bytes 16 | tf_op jit(solution)/shard_map/psum | solution.py:82
  542.2 6.5 multiply_reduce_fusion.3
  548.7 30.1 %psum.148 = f32[]{:T(128)} all-reduce(f32[]{:T(128)} %multiply_reduce_fusion.3), channel_id=1, replica_groups=mesh['groups'=2,'fsdp'=8,'dp'=2] {'fsdp','dp'}, use_global_device_ids=true, to_apply=%region_21.0 | all-reduce | flops 1 | bytes 8 | tf_op jit(solution)/shard_map/psum | solution.py:82
  580.0 8.2 fusion.15
  588.4 18.3 %all-gather.16.cloned.1.call-done = bf16[6912,640]{0,1:T(8,128)(2,1)} async-done(((bf16[3456,640]{0,1:T(8,128)(2,1)}), bf16[6912,640]{0,1:T(8,128)(2,1)}) %all-gather.16.cloned.1.call-update) | async-done | bytes 8847376 | tf_op jit(solution)/shard_map/all_gather | solution.py:68
  606.7 6.4 multiply_reduce_fusion.6
  613.1 21.6 %psum.149 = f32[128,1]{0,1:T(1,128)S(1)} all-reduce(f32[128,1]{0,1:T(1,128)S(1)} %bitcast.135), channel_id=1, replica_groups=mesh['groups'=2,'fsdp'=8,'dp'=2] {'fsdp'}, use_global_device_ids=true, to_apply=%region_23.0 | all-reduce | flops 128 | bytes 1024 | tf_op jit(solution)/shard_map/psum | solution.py:13
  635.6 39.9 %all-gather.18.cloned.1.call-done = bf16[128,5120]{1,0:T(8,128)(2,1)} async-done(((bf16[128,640]{1,0:T(8,128)(2,1)}), bf16[128,5120]{1,0:T(8,128)(2,1)}) %all-gather.18.cloned.1.call-update) | async-done | bytes 1310736 | tf_op jit(solution)/shard_map/all_gather | solution.py:29
  675.5 11.6 fusion.83
  687.0 19.1 %psum.150 = f32[128]{0:T(128)S(1)} all-reduce(f32[128]{0:T(128)S(1)} %get-tuple-element.25), channel_id=1, replica_groups=mesh['groups'=2,'fsdp'=8,'dp'=2] {'fsdp'}, use_global_device_ids=true, to_apply=%region_25.0 | all-reduce | flops 128 | bytes 1024 | tf_op jit(solution)/shard_map/psum | solution.py:13
  706.1 11.9 fusion.13
  719.5 62.5 %reduce-scatter.33.cloned.1.call-done = bf16[640,128]{1,0:T(8,128)(2,1)} async-done(((bf16[5120,128]{1,0:T(8,128)(2,1)}), bf16[640,128]{1,0:T(8,128)(2,1)}) %reduce-scatter.33.cloned.1.call-update) | async-done | bytes 163856
  783.3 19.1 %psum.151 = f32[128,1]{0,1:T(1,128)S(1)} all-reduce(f32[128,1]{0,1:T(1,128)S(1)} %bitcast.132), channel_id=1, replica_groups=mesh['groups'=2,'fsdp'=8,'dp'=2] {'fsdp'}, use_global_device_ids=true, to_apply=%region_28.0 | all-reduce | flops 128 | bytes 1024 | tf_op jit(solution)/shard_map/psum | solution.py:13
  808.4 12.6 copy.30
  821.1 14.1 %reduce-scatter.35.cloned.1.call-done = bf16[3456,640]{1,0:T(8,128)(2,1)} async-done(((bf16[6912,640]{1,0:T(8,128)(2,1)}), bf16[3456,640]{1,0:T(8,128)(2,1)}) %reduce-scatter.35.cloned.1.call-update) | async-done | bytes 4423696
  835.1 7.2 copy.31
  842.3 7.3 multiply_reduce_fusion.2
  849.7 34.5 %psum.152 = f32[]{:T(128)} all-reduce(f32[]{:T(128)} %multiply_reduce_fusion.2), channel_id=1, replica_groups=mesh['groups'=2,'fsdp'=8,'dp'=2] {'fsdp','dp'}, use_global_device_ids=true, to_apply=%region_31.0 | all-reduce | flops 1 | bytes 8 | tf_op jit(solution)/shard_map/psum | solution.py:82
  885.5 7.9 multiply_reduce_fusion.1
  893.3 30.3 %psum.153 = f32[]{:T(128)} all-reduce(f32[]{:T(128)} %multiply_reduce_fusion.1), channel_id=1, replica_groups=mesh['groups'=2,'fsdp'=8,'dp'=2] {'fsdp','dp'}, use_global_device_ids=true, to_apply=%region_33.0 | all-reduce | flops 1 | bytes 8 | tf_op jit(solution)/shard_map/psum | solution.py:82
  924.9 10.2 fusion.80
  935.1 18.4 %all-gather.20.cloned.1.call-done = bf16[6912,640]{0,1:T(8,128)(2,1)} async-done(((bf16[3456,640]{0,1:T(8,128)(2,1)}), bf16[6912,640]{0,1:T(8,128)(2,1)}) %all-gather.20.cloned.1.call-update) | async-done | bytes 8847376 | tf_op jit(solution)/shard_map/all_gather | solution.py:68
  953.5 6.4 multiply_reduce_fusion.5
  959.9 21.6 %psum.154 = f32[128,1]{0,1:T(1,128)S(1)} all-reduce(f32[128,1]{0,1:T(1,128)S(1)} %bitcast.136), channel_id=1, replica_groups=mesh['groups'=2,'fsdp'=8,'dp'=2] {'fsdp'}, use_global_device_ids=true, to_apply=%region_35.0 | all-reduce | flops 128 | bytes 1024 | tf_op jit(solution)/shard_map/psum | solution.py:13
  982.4 39.9 %all-gather.22.cloned.1.call-done = bf16[128,5120]{1,0:T(8,128)(2,1)} async-done(((bf16[128,640]{1,0:T(8,128)(2,1)}), bf16[128,5120]{1,0:T(8,128)(2,1)}) %all-gather.22.cloned.1.call-update) | async-done | bytes 1310736 | tf_op jit(solution)/shard_map/all_gather | solution.py:29
  1022.2 11.5 fusion.84
  1033.8 19.0 %psum.155 = f32[128]{0:T(128)S(1)} all-reduce(f32[128]{0:T(128)S(1)} %get-tuple-element.29), channel_id=1, replica_groups=mesh['groups'=2,'fsdp'=8,'dp'=2] {'fsdp'}, use_global_device_ids=true, to_apply=%region_37.0 | all-reduce | flops 128 | bytes 1024 | tf_op jit(solution)/shard_map/psum | solution.py:13
  1052.7 11.8 fusion.14
  1066.1 62.5 %reduce-scatter.37.cloned.1.call-done = bf16[640,128]{1,0:T(8,128)(2,1)} async-done(((bf16[5120,128]{1,0:T(8,128)(2,1)}), bf16[640,128]{1,0:T(8,128)(2,1)}) %reduce-scatter.37.cloned.1.call-update) | async-done | bytes 163856
  1129.7 19.5 %psum.156 = f32[128,1]{0,1:T(1,128)S(1)} all-reduce(f32[128,1]{0,1:T(1,128)S(1)} %bitcast.133), channel_id=1, replica_groups=mesh['groups'=2,'fsdp'=8,'dp'=2] {'fsdp'}, use_global_device_ids=true, to_apply=%region_40.0 | all-reduce | flops 128 | bytes 1024 | tf_op jit(solution)/shard_map/psum | solution.py:13
  1155.3 12.5 copy.34
  1167.8 14.0 %reduce-scatter.39.cloned.1.call-done = bf16[3456,640]{1,0:T(8,128)(2,1)} async-done(((bf16[6912,640]{1,0:T(8,128)(2,1)}), bf16[3456,640]{1,0:T(8,128)(2,1)}) %reduce-scatter.39.cloned.1.call-update) | async-done | bytes 4423696
  1181.9 7.2 copy.35
  1189.1 7.7 multiply_reduce_fusion
  1196.7 34.5 %psum.157 = f32[]{:T(128)} all-reduce(f32[]{:T(128)} %multiply_reduce_fusion), channel_id=1, replica_groups=mesh['groups'=2,'fsdp'=8,'dp'=2] {'fsdp','dp'}, use_global_device_ids=true, to_apply=%region_43.0 | all-reduce | flops 1 | bytes 8 | tf_op jit(solution)/shard_map/psum | solution.py:82
  1232.5 9.5 fusion.9
  1242.1 18.3 %all-gather.24.cloned.1.call-done = bf16[6912,640]{0,1:T(8,128)(2,1)} async-done(((bf16[3456,640]{0,1:T(8,128)(2,1)}), bf16[6912,640]{0,1:T(8,128)(2,1)}) %all-gather.24.cloned.1.call-update) | async-done | bytes 8847376 | tf_op jit(solution)/shard_map/all_gather | solution.py:68
  1260.4 6.4 multiply_reduce_fusion.4
  1266.8 21.9 %psum.158 = f32[128,1]{0,1:T(1,128)S(1)} all-reduce(f32[128,1]{0,1:T(1,128)S(1)} %bitcast.137), channel_id=1, replica_groups=mesh['groups'=2,'fsdp'=8,'dp'=2] {'fsdp'}, use_global_device_ids=true, to_apply=%region_45.0 | all-reduce | flops 128 | bytes 1024 | tf_op jit(solution)/shard_map/psum | solution.py:13
  1289.5 39.9 %all-gather.26.cloned.1.call-done = bf16[128,5120]{1,0:T(8,128)(2,1)} async-done(((bf16[128,640]{1,0:T(8,128)(2,1)}), bf16[128,5120]{1,0:T(8,128)(2,1)}) %all-gather.26.cloned.1.call-update) | async-done | bytes 1310736 | tf_op jit(solution)/shard_map/all_gather | solution.py:29
  1329.4 10.8 fusion.21
  1340.2 19.5 %psum.159 = f32[128]{0:T(128)} all-reduce(f32[128]{0:T(128)S(1)} %fusion.21), channel_id=1, replica_groups=mesh['groups'=2,'fsdp'=8,'dp'=2] {'fsdp'}, use_global_device_ids=true, to_apply=%region_47.0 | all-reduce | flops 128 | bytes 1024 | tf_op jit(solution)/shard_map/psum | solution.py:13
  (86 shorter events, 52.4 us)
Async XLA Ops:
  6.5 1.5 copy-start
  6.5 70.6 %all-gather.10.cloned.1.call-start = ((), (), s32[]{:S(2)}) async-start(), calls=%async_computation.8 | async-start | bytes 1474560 | tf_op jit(solution)/shard_map/all_gather | solution.py:29
  37.1 145.9 %reduce-scatter.25.cloned.1.call-start = ((), (), s32[]{:S(2)}) async-start(), calls=%async_computation.17 | async-start | bytes 1474560
  37.2 70.2 %copy-start.5 = (s32[2048]{0:T(1024)}, s32[2048]{0:T(1024)S(1)}, u32[]{:S(2)}) copy-start(s32[2048]{0:T(1024)S(1)} %iota_add_fusion) | copy-start | bytes 24580
  37.2 70.2 %copy-start.7 = (s32[128]{0:T(128)S(1)}, s32[128]{0:T(128)}, u32[]{:S(2)}) copy-start(s32[128]{0:T(128)} %param.13) | copy-start | bytes 1540
  120.4 115.6 %reduce-scatter.27.cloned.1.call-start = ((), (), s32[]{:S(2)}) async-start(), calls=%async_computation.18 | async-start | bytes 13271040
  221.9 43.8 %all-gather.12.cloned.1.call-start = ((), (), s32[]{:S(2)}) async-start(), calls=%async_computation.9 | async-start | bytes 13271040 | tf_op jit(solution)/shard_map/all_gather | solution.py:68
  243.2 91.2 %copy-start.1 = (f32[128,2048]{1,0:T(8,128)S(1)}, f32[128,2048]{1,0:T(8,128)}, u32[]{:S(2)}) copy-start(f32[128,2048]{1,0:T(8,128)} %get-tuple-element.18) | copy-start | bytes 3145732
  243.3 91.2 %all-gather.14.cloned.1.call-start = ((), (), s32[]{:S(2)}) async-start(), calls=%async_computation.10 | async-start | bytes 1474560 | tf_op jit(solution)/shard_map/all_gather | solution.py:29
  294.5 146.3 %reduce-scatter.29.cloned.1.call-start = ((), (), s32[]{:S(2)}) async-start(), calls=%async_computation.19 | async-start | bytes 1474560
  378.4 115.5 %reduce-scatter.31.cloned.1.call-start = ((), (), s32[]{:S(2)}) async-start(), calls=%async_computation.20 | async-start | bytes 13271040
  479.9 126.8 %all-gather.16.cloned.1.call-start = ((), (), s32[]{:S(2)}) async-start(), calls=%async_computation.11 | async-start | bytes 13271040 | tf_op jit(solution)/shard_map/all_gather | solution.py:68
  588.3 87.2 %copy-start.2 = (f32[128,2048]{1,0:T(8,128)S(1)}, f32[128,2048]{1,0:T(8,128)}, u32[]{:S(2)}) copy-start(f32[128,2048]{1,0:T(8,128)} %get-tuple-element.18) | copy-start | bytes 3145732
  588.3 87.2 %all-gather.18.cloned.1.call-start = ((), (), s32[]{:S(2)}) async-start(), calls=%async_computation.12 | async-start | bytes 1474560 | tf_op jit(solution)/shard_map/all_gather | solution.py:29
  635.5 146.6 %reduce-scatter.33.cloned.1.call-start = ((), (), s32[]{:S(2)}) async-start(), calls=%async_computation.21 | async-start | bytes 1474560
  719.5 115.6 %reduce-scatter.35.cloned.1.call-start = ((), (), s32[]{:S(2)}) async-start(), calls=%async_computation.22 | async-start | bytes 13271040
  821.0 132.5 %all-gather.20.cloned.1.call-start = ((), (), s32[]{:S(2)}) async-start(), calls=%async_computation.13 | async-start | bytes 13271040 | tf_op jit(solution)/shard_map/all_gather | solution.py:68
  935.1 87.2 %copy-start.3 = (f32[128,2048]{1,0:T(8,128)S(1)}, f32[128,2048]{1,0:T(8,128)}, u32[]{:S(2)}) copy-start(f32[128,2048]{1,0:T(8,128)} %get-tuple-element.18) | copy-start | bytes 3145732
  935.1 87.2 %all-gather.22.cloned.1.call-start = ((), (), s32[]{:S(2)}) async-start(), calls=%async_computation.14 | async-start | bytes 1474560 | tf_op jit(solution)/shard_map/all_gather | solution.py:29
  982.3 146.2 %reduce-scatter.37.cloned.1.call-start = ((), (), s32[]{:S(2)}) async-start(), calls=%async_computation.23 | async-start | bytes 1474560
  1066.0 115.9 %reduce-scatter.39.cloned.1.call-start = ((), (), s32[]{:S(2)}) async-start(), calls=%async_computation.24 | async-start | bytes 13271040
  1167.8 92.6 %all-gather.24.cloned.1.call-start = ((), (), s32[]{:S(2)}) async-start(), calls=%async_computation.15 | async-start | bytes 13271040 | tf_op jit(solution)/shard_map/all_gather | solution.py:68
  1242.0 87.5 %copy-start.4 = (f32[128,2048]{1,0:T(8,128)S(1)}, f32[128,2048]{1,0:T(8,128)}, u32[]{:S(2)}) copy-start(f32[128,2048]{1,0:T(8,128)} %get-tuple-element.18) | copy-start | bytes 3145732
  1242.0 87.5 %copy-start.6 = (s32[2048]{0:T(1024)S(1)}, s32[2048]{0:T(1024)}, u32[]{:S(2)}) copy-start(s32[2048]{0:T(1024)} %copy-done.5) | copy-start | bytes 24580
  1242.0 87.5 %copy-start.8 = (s32[128]{0:T(128)S(1)}, s32[128]{0:T(128)}, u32[]{:S(2)}) copy-start(s32[128]{0:T(128)} %param.12) | copy-start | bytes 1540
  1242.0 87.4 %all-gather.26.cloned.1.call-start = ((), (), s32[]{:S(2)}) async-start(), calls=%async_computation.16 | async-start | bytes 1474560 | tf_op jit(solution)/shard_map/all_gather | solution.py:29
Sparse Core Ops, SparseCore 0:
  37.2 39.7 all-gather.9
  120.5 62.4 reduce-scatter.24
  222.0 13.9 reduce-scatter.26
  243.4 22.2 all-gather.11
  294.6 39.7 all-gather.13
  378.5 62.3 reduce-scatter.28
  480.0 13.8 reduce-scatter.30
  588.4 18.2 all-gather.15
  635.6 39.7 all-gather.17
  719.6 62.4 reduce-scatter.32
  821.1 13.9 reduce-scatter.34
  935.2 18.2 all-gather.19
  982.4 39.7 all-gather.21
  1066.1 62.3 reduce-scatter.36
  1167.9 13.9 reduce-scatter.38
  1242.1 18.2 all-gather.23
  1289.6 39.7 all-gather.25
where the time goes:
time: 1380 us; the launch traced here: 1370 us
  waiting for transfers between devices  583 us (42%)
  blocking collectives  446 us (32%)
  matrix products  159 us (12%)
  local copies, waits for them, and re-layouts  89.8 us (7%)
  other arithmetic  68 us (5%)
  between operations  20.3 us (1%)
    unnamed x25, waiting for transfers between devices  306 us
    psum x14, blocking collectives, row_total(): return lax.psum(values, 'fsdp')  282 us
    all_gather x5, waiting for transfers between devices, head_logits(): lax.all_gather(normed_shard, 'fsdp', axis=1, tiled=True)  199 us
    psum x5, blocking collectives, global_dot(): return lax.psum(values, ('fsdp', 'dp'))  164 us
    unnamed x34, local copies, waits for them, and re-layouts  89.8 us
    all_gather x4, waiting for transfers between devices, full_rows(): return lax.all_gather(vector.astype(jnp.bfloat16), 'dp', axis=0, tiled=True)  77.2 us
    dot_general x5, matrix products, head_logits(): jnp.dot(lax.all_gather(normed_shard, 'fsdp', axis=1, tiled=True), head, p...  56.8 us
    dot_general x4, matrix products, head_project(): lax.dot_general(head, weighted, (((1,), (1,)), ((), ())), preferred_eleme...  47 us
  transfers between devices with their start and end apart: 17, of which 17 were waited for; matrix products, arithmetic and copies ran while one was open for 0% of the time, Pallas kernels for 0%

commit v1 on v0

--- a/solution.py
+++ b/solution.py
@@ -7,6 +7,12 @@
 cap_value = 30.0
 norm_eps = 1e-05
 damping = 0.05
+
+
+def gather_and_add(x, mesh_axis):
+    parts = lax.all_gather(x, mesh_axis, axis=0, tiled=False)
+    acc = parts.sum(axis=0)
+    return acc
 
 
 def row_total(values):
@@ -79,7 +85,7 @@
         ).astype(jnp.float32)
 
     def global_dot(values):
-        return lax.psum(values, ("fsdp", "dp"))
+        return gather_and_add(values, ("fsdp", "dp"))
 
     pseudo_hot = (pseudo_ids[:, None] == vocab_ids).astype(jnp.float32)
     grad = param_sum(norm_back((prob - pseudo_hot) / total_rows))

time: 1380 us -> 1390 us (level)
    psum x5 -> x0, blocking collectives: 164 us -> none  [global_dot(): return lax.psum(values, ('fsdp', 'dp'))]
    unnamed x0 -> x5, blocking collectives: none -> 161 us
    unnamed x34 -> x49, local copies, waits for them, and re-layouts: 89.8 us -> 98.8 us
where the time goes in v1:
time: 1390 us; the launch traced here: 1370 us
  waiting for transfers between devices  581 us (42%)
  blocking collectives  442 us (32%)
  matrix products  159 us (11%)
  local copies, waits for them, and re-layouts  98.8 us (7%)
  other arithmetic  71.9 us (5%)
  between operations  20.3 us (1%)
    unnamed x25, waiting for transfers between devices  305 us
    psum x14, blocking collectives, row_total(): return lax.psum(values, 'fsdp')  282 us
    all_gather x5, waiting for transfers between devices, head_logits(): lax.all_gather(normed_shard, 'fsdp', axis=1, tiled=True)  199 us
    unnamed x5, blocking collectives  161 us
    unnamed x49, local copies, waits for them, and re-layouts  98.8 us
    all_gather x4, waiting for transfers between devices, full_rows(): return lax.all_gather(vector.astype(jnp.bfloat16), 'dp', axis=0, tiled=True)  76.8 us
    dot_general x5, matrix products, head_logits(): jnp.dot(lax.all_gather(normed_shard, 'fsdp', axis=1, tiled=True), head, p...  56.8 us
    dot_general x4, matrix products, head_project(): lax.dot_general(head, weighted, (((1,), (1,)), ((), ())), preferred_eleme...  47 us
  transfers between devices with their start and end apart: 17, of which 17 were waited for; matrix products, arithmetic and copies ran while one was open for 0% of the time, Pallas kernels for 0%

profile of v1, /device:TPU:0, one launch (start us, length us, event | category | flops | bytes accessed | tf_op | source)
XLA Modules:
  0.0 1374.9 jit_solution(4984758867359583961)
XLA Ops:
  13.2 23.2 %psum.98 = f32[128,1]{0,1:T(1,128)S(1)} all-reduce(f32[128,1]{0,1:T(1,128)S(1)} %bitcast.136), channel_id=1, replica_groups=mesh['groups'=2,'fsdp'=8,'dp'=2] {'fsdp'}, use_global_device_ids=true, to_apply=%region_1.0 | all-reduce | flops 128 | bytes 1024 | tf_op jit(solution)/shard_map/psum | solution.py:19
  37.2 39.9 %all-gather.10.cloned.1.call-done = bf16[128,5120]{1,0:T(8,128)(2,1)} async-done(((bf16[128,640]{1,0:T(8,128)(2,1)}), bf16[128,5120]{1,0:T(8,128)(2,1)}) %all-gather.10.cloned.1.call-update) | async-done | bytes 1310736 | tf_op jit(solution)/shard_map/all_gather | solution.py:35
  77.1 11.3 fusion.23
  88.4 19.0 %psum.99 = f32[128]{0:T(128)S(1)} all-reduce(f32[128]{0:T(128)S(1)} %get-tuple-element.17), channel_id=1, replica_groups=mesh['groups'=2,'fsdp'=8,'dp'=2] {'fsdp'}, use_global_device_ids=true, to_apply=%region_3.0 | all-reduce | flops 128 | bytes 1024 | tf_op jit(solution)/shard_map/psum | solution.py:19
  107.4 11.5 fusion.11
  120.4 62.4 %reduce-scatter.25.cloned.1.call-done = bf16[640,128]{1,0:T(8,128)(2,1)} async-done(((bf16[5120,128]{1,0:T(8,128)(2,1)}), bf16[640,128]{1,0:T(8,128)(2,1)}) %reduce-scatter.25.cloned.1.call-update) | async-done | bytes 163856
  184.1 19.1 %psum.100 = f32[128,1]{0,1:T(1,128)S(1)} all-reduce(f32[128,1]{0,1:T(1,128)S(1)} %bitcast.137), channel_id=1, replica_groups=mesh['groups'=2,'fsdp'=8,'dp'=2] {'fsdp'}, use_global_device_ids=true, to_apply=%region_6.0 | all-reduce | flops 128 | bytes 1024 | tf_op jit(solution)/shard_map/psum | solution.py:19
  209.2 12.6 copy.22
  221.8 14.1 %reduce-scatter.27.cloned.1.call-done = bf16[3456,640]{1,0:T(8,128)(2,1)} async-done(((bf16[6912,640]{1,0:T(8,128)(2,1)}), bf16[3456,640]{1,0:T(8,128)(2,1)}) %reduce-scatter.27.cloned.1.call-update) | async-done | bytes 4423696
  235.9 7.2 copy.23
  243.6 21.9 %all-gather.12.cloned.1.call-done = bf16[6912,640]{0,1:T(8,128)(2,1)} async-done(((bf16[3456,640]{0,1:T(8,128)(2,1)}), bf16[6912,640]{0,1:T(8,128)(2,1)}) %all-gather.12.cloned.1.call-update) | async-done | bytes 8847376 | tf_op jit(solution)/shard_map/all_gather | solution.py:74
  265.6 6.4 multiply_reduce_fusion.7
  271.9 21.6 %psum.101 = f32[128,1]{0,1:T(1,128)S(1)} all-reduce(f32[128,1]{0,1:T(1,128)S(1)} %bitcast.141), channel_id=1, replica_groups=mesh['groups'=2,'fsdp'=8,'dp'=2] {'fsdp'}, use_global_device_ids=true, to_apply=%region_11.0 | all-reduce | flops 128 | bytes 1024 | tf_op jit(solution)/shard_map/psum | solution.py:19
  294.5 39.9 %all-gather.14.cloned.1.call-done = bf16[128,5120]{1,0:T(8,128)(2,1)} async-done(((bf16[128,640]{1,0:T(8,128)(2,1)}), bf16[128,5120]{1,0:T(8,128)(2,1)}) %all-gather.14.cloned.1.call-update) | async-done | bytes 1310736 | tf_op jit(solution)/shard_map/all_gather | solution.py:35
  334.4 11.5 fusion.82
  345.9 19.0 %psum.102 = f32[128]{0:T(128)S(1)} all-reduce(f32[128]{0:T(128)S(1)} %get-tuple-element.21), channel_id=1, replica_groups=mesh['groups'=2,'fsdp'=8,'dp'=2] {'fsdp'}, use_global_device_ids=true, to_apply=%region_13.0 | all-reduce | flops 128 | bytes 1024 | tf_op jit(solution)/shard_map/psum | solution.py:19
  364.9 11.9 fusion.12
  378.3 62.5 %reduce-scatter.29.cloned.1.call-done = bf16[640,128]{1,0:T(8,128)(2,1)} async-done(((bf16[5120,128]{1,0:T(8,128)(2,1)}), bf16[640,128]{1,0:T(8,128)(2,1)}) %reduce-scatter.29.cloned.1.call-update) | async-done | bytes 163856
  441.9 19.2 %psum.103 = f32[128,1]{0,1:T(1,128)S(1)} all-reduce(f32[128,1]{0,1:T(1,128)S(1)} %bitcast.138), channel_id=1, replica_groups=mesh['groups'=2,'fsdp'=8,'dp'=2] {'fsdp'}, use_global_device_ids=true, to_apply=%region_16.0 | all-reduce | flops 128 | bytes 1024 | tf_op jit(solution)/shard_map/psum | solution.py:19
  467.2 12.6 copy.26
  481.0 12.8 reduce-scatter.31.cloned.1.call-done
  493.8 7.2 copy.27
  509.1 33.8 %all-reduce.6 = (f32[16]{0:T(128)S(1)}, f32[16]{0:T(128)S(1)}) all-reduce(f32[16]{0:T(128)S(1)} %dynamic-update-slice, f32[16]{0:T(128)S(1)} %dynamic-update-slice.1), channel_id=1, replica_groups=mesh['groups'=2,'fsdp'=8,'dp'=2] {'fsdp','dp'}, use_global_device_ids=true, to_apply=%add | all-reduce | flops 32 | bytes 256
  545.6 6.6 multiply_reduce_fusion.3
  553.5 29.5 %all-reduce.2 = f32[16]{0:T(128)S(1)} all-reduce(f32[16]{0:T(128)S(1)} %dynamic-update-slice.2), channel_id=1, replica_groups=mesh['groups'=2,'fsdp'=8,'dp'=2] {'fsdp','dp'}, use_global_device_ids=true, to_apply=%add.2 | all-reduce | flops 16 | bytes 128
  584.9 8.2 fusion.15
  593.2 18.3 %all-gather.16.cloned.1.call-done = bf16[6912,640]{0,1:T(8,128)(2,1)} async-done(((bf16[3456,640]{0,1:T(8,128)(2,1)}), bf16[6912,640]{0,1:T(8,128)(2,1)}) %all-gather.16.cloned.1.call-update) | async-done | bytes 8847376 | tf_op jit(solution)/shard_map/all_gather | solution.py:74
  611.6 6.4 multiply_reduce_fusion.6
  617.9 21.6 %psum.104 = f32[128,1]{0,1:T(1,128)S(1)} all-reduce(f32[128,1]{0,1:T(1,128)S(1)} %bitcast.142), channel_id=1, replica_groups=mesh['groups'=2,'fsdp'=8,'dp'=2] {'fsdp'}, use_global_device_ids=true, to_apply=%region_23.0 | all-reduce | flops 128 | bytes 1024 | tf_op jit(solution)/shard_map/psum | solution.py:19
  640.6 39.7 %all-gather.18.cloned.1.call-done = bf16[128,5120]{1,0:T(8,128)(2,1)} async-done(((bf16[128,640]{1,0:T(8,128)(2,1)}), bf16[128,5120]{1,0:T(8,128)(2,1)}) %all-gather.18.cloned.1.call-update) | async-done | bytes 1310736 | tf_op jit(solution)/shard_map/all_gather | solution.py:35
  680.3 11.6 fusion.83
  691.9 19.0 %psum.105 = f32[128]{0:T(128)S(1)} all-reduce(f32[128]{0:T(128)S(1)} %get-tuple-element.25), channel_id=1, replica_groups=mesh['groups'=2,'fsdp'=8,'dp'=2] {'fsdp'}, use_global_device_ids=true, to_apply=%region_25.0 | all-reduce | flops 128 | bytes 1024 | tf_op jit(solution)/shard_map/psum | solution.py:19
  710.9 11.9 fusion.13
  724.2 62.4 %reduce-scatter.33.cloned.1.call-done = bf16[640,128]{1,0:T(8,128)(2,1)} async-done(((bf16[5120,128]{1,0:T(8,128)(2,1)}), bf16[640,128]{1,0:T(8,128)(2,1)}) %reduce-scatter.33.cloned.1.call-update) | async-done | bytes 163856
  787.8 19.1 %psum.106 = f32[128,1]{0,1:T(1,128)S(1)} all-reduce(f32[128,1]{0,1:T(1,128)S(1)} %bitcast.139), channel_id=1, replica_groups=mesh['groups'=2,'fsdp'=8,'dp'=2] {'fsdp'}, use_global_device_ids=true, to_apply=%region_28.0 | all-reduce | flops 128 | bytes 1024 | tf_op jit(solution)/shard_map/psum | solution.py:19
  813.0 12.6 copy.30
  825.7 14.0 %reduce-scatter.35.cloned.1.call-done = bf16[3456,640]{1,0:T(8,128)(2,1)} async-done(((bf16[6912,640]{1,0:T(8,128)(2,1)}), bf16[3456,640]{1,0:T(8,128)(2,1)}) %reduce-scatter.35.cloned.1.call-update) | async-done | bytes 4423696
  839.7 7.2 copy.31
  846.9 7.3 multiply_reduce_fusion.2
  855.5 34.2 %all-reduce.3 = f32[16]{0:T(128)S(1)} all-reduce(f32[16]{0:T(128)S(1)} %dynamic-update-slice.3), channel_id=1, replica_groups=mesh['groups'=2,'fsdp'=8,'dp'=2] {'fsdp','dp'}, use_global_device_ids=true, to_apply=%add.3 | all-reduce | flops 16 | bytes 128
  891.7 7.9 multiply_reduce_fusion.1
  900.9 29.5 %all-reduce.4 = f32[16]{0:T(128)S(1)} all-reduce(f32[16]{0:T(128)S(1)} %dynamic-update-slice.4), channel_id=1, replica_groups=mesh['groups'=2,'fsdp'=8,'dp'=2] {'fsdp','dp'}, use_global_device_ids=true, to_apply=%add.4 | all-reduce | flops 16 | bytes 128
  932.3 10.2 fusion.80
  942.5 18.4 %all-gather.20.cloned.1.call-done = bf16[6912,640]{0,1:T(8,128)(2,1)} async-done(((bf16[3456,640]{0,1:T(8,128)(2,1)}), bf16[6912,640]{0,1:T(8,128)(2,1)}) %all-gather.20.cloned.1.call-update) | async-done | bytes 8847376 | tf_op jit(solution)/shard_map/all_gather | solution.py:74
  960.8 6.4 multiply_reduce_fusion.5
  967.2 21.6 %psum.107 = f32[128,1]{0,1:T(1,128)S(1)} all-reduce(f32[128,1]{0,1:T(1,128)S(1)} %bitcast.143), channel_id=1, replica_groups=mesh['groups'=2,'fsdp'=8,'dp'=2] {'fsdp'}, use_global_device_ids=true, to_apply=%region_35.0 | all-reduce | flops 128 | bytes 1024 | tf_op jit(solution)/shard_map/psum | solution.py:19
  989.7 39.9 %all-gather.22.cloned.1.call-done = bf16[128,5120]{1,0:T(8,128)(2,1)} async-done(((bf16[128,640]{1,0:T(8,128)(2,1)}), bf16[128,5120]{1,0:T(8,128)(2,1)}) %all-gather.22.cloned.1.call-update) | async-done | bytes 1310736 | tf_op jit(solution)/shard_map/all_gather | solution.py:35
  1029.6 11.5 fusion.84
  1041.1 19.1 %psum.108 = f32[128]{0:T(128)S(1)} all-reduce(f32[128]{0:T(128)S(1)} %get-tuple-element.29), channel_id=1, replica_groups=mesh['groups'=2,'fsdp'=8,'dp'=2] {'fsdp'}, use_global_device_ids=true, to_apply=%region_37.0 | all-reduce | flops 128 | bytes 1024 | tf_op jit(solution)/shard_map/psum | solution.py:19
  1060.3 11.8 fusion.14
  1073.6 62.5 %reduce-scatter.37.cloned.1.call-done = bf16[640,128]{1,0:T(8,128)(2,1)} async-done(((bf16[5120,128]{1,0:T(8,128)(2,1)}), bf16[640,128]{1,0:T(8,128)(2,1)}) %reduce-scatter.37.cloned.1.call-update) | async-done | bytes 163856
  1137.3 19.1 %psum.109 = f32[128,1]{0,1:T(1,128)S(1)} all-reduce(f32[128,1]{0,1:T(1,128)S(1)} %bitcast.140), channel_id=1, replica_groups=mesh['groups'=2,'fsdp'=8,'dp'=2] {'fsdp'}, use_global_device_ids=true, to_apply=%region_40.0 | all-reduce | flops 128 | bytes 1024 | tf_op jit(solution)/shard_map/psum | solution.py:19
  1162.5 12.5 copy.34
  1175.0 14.0 %reduce-scatter.39.cloned.1.call-done = bf16[3456,640]{1,0:T(8,128)(2,1)} async-done(((bf16[6912,640]{1,0:T(8,128)(2,1)}), bf16[3456,640]{1,0:T(8,128)(2,1)}) %reduce-scatter.39.cloned.1.call-update) | async-done | bytes 4423696
  1189.1 7.2 copy.35
  1196.3 7.7 multiply_reduce_fusion
  1205.3 33.8 %all-reduce.5 = f32[16]{0:T(128)S(1)} all-reduce(f32[16]{0:T(128)S(1)} %dynamic-update-slice.5), channel_id=1, replica_groups=mesh['groups'=2,'fsdp'=8,'dp'=2] {'fsdp','dp'}, use_global_device_ids=true, to_apply=%add.5 | all-reduce | flops 16 | bytes 128
  1241.1 9.5 fusion.9
  1250.9 18.1 %all-gather.24.cloned.1.call-done = bf16[6912,640]{0,1:T(8,128)(2,1)} async-done(((bf16[3456,640]{0,1:T(8,128)(2,1)}), bf16[6912,640]{0,1:T(8,128)(2,1)}) %all-gather.24.cloned.1.call-update) | async-done | bytes 8847376 | tf_op jit(solution)/shard_map/all_gather | solution.py:74
  1269.1 6.4 multiply_reduce_fusion.4
  1275.4 21.6 %psum.110 = f32[128,1]{0,1:T(1,128)S(1)} all-reduce(f32[128,1]{0,1:T(1,128)S(1)} %bitcast.144), channel_id=1, replica_groups=mesh['groups'=2,'fsdp'=8,'dp'=2] {'fsdp'}, use_global_device_ids=true, to_apply=%region_45.0 | all-reduce | flops 128 | bytes 1024 | tf_op jit(solution)/shard_map/psum | solution.py:19
  1297.9 39.9 %all-gather.26.cloned.1.call-done = bf16[128,5120]{1,0:T(8,128)(2,1)} async-done(((bf16[128,640]{1,0:T(8,128)(2,1)}), bf16[128,5120]{1,0:T(8,128)(2,1)}) %all-gather.26.cloned.1.call-update) | async-done | bytes 1310736 | tf_op jit(solution)/shard_map/all_gather | solution.py:35
  1337.8 10.8 fusion.21
  1348.6 19.5 %psum.111 = f32[128]{0:T(128)} all-reduce(f32[128]{0:T(128)S(1)} %fusion.21), channel_id=1, replica_groups=mesh['groups'=2,'fsdp'=8,'dp'=2] {'fsdp'}, use_global_device_ids=true, to_apply=%region_47.0 | all-reduce | flops 128 | bytes 1024 | tf_op jit(solution)/shard_map/psum | solution.py:19
  (107 shorter events, 65.7 us)
Async XLA Ops:
  6.5 1.5 copy-start
  6.5 70.6 %all-gather.10.cloned.1.call-start = ((), (), s32[]{:S(2)}) async-start(), calls=%async_computation.8 | async-start | bytes 1474560 | tf_op jit(solution)/shard_map/all_gather | solution.py:35
  37.1 145.8 %reduce-scatter.25.cloned.1.call-start = ((), (), s32[]{:S(2)}) async-start(), calls=%async_computation.17 | async-start | bytes 1474560
  37.2 70.2 %copy-start.5 = (s32[2048]{0:T(1024)}, s32[2048]{0:T(1024)S(1)}, u32[]{:S(2)}) copy-start(s32[2048]{0:T(1024)S(1)} %iota_add_fusion) | copy-start | bytes 24580
  37.2 70.2 %copy-start.7 = (s32[128]{0:T(128)S(1)}, s32[128]{0:T(128)}, u32[]{:S(2)}) copy-start(s32[128]{0:T(128)} %param.13) | copy-start | bytes 1540
  120.4 115.5 %reduce-scatter.27.cloned.1.call-start = ((), (), s32[]{:S(2)}) async-start(), calls=%async_computation.18 | async-start | bytes 13271040
  221.8 43.8 %all-gather.12.cloned.1.call-start = ((), (), s32[]{:S(2)}) async-start(), calls=%async_computation.9 | async-start | bytes 13271040 | tf_op jit(solution)/shard_map/all_gather | solution.py:74
  243.1 91.3 %copy-start.1 = (f32[128,2048]{1,0:T(8,128)S(1)}, f32[128,2048]{1,0:T(8,128)}, u32[]{:S(2)}) copy-start(f32[128,2048]{1,0:T(8,128)} %get-tuple-element.18) | copy-start | bytes 3145732
  243.1 91.2 %all-gather.14.cloned.1.call-start = ((), (), s32[]{:S(2)}) async-start(), calls=%async_computation.10 | async-start | bytes 1474560 | tf_op jit(solution)/shard_map/all_gather | solution.py:35
  294.4 146.3 %reduce-scatter.29.cloned.1.call-start = ((), (), s32[]{:S(2)}) async-start(), calls=%async_computation.19 | async-start | bytes 1474560
  378.2 115.5 %reduce-scatter.31.cloned.1.call-start = ((), (), s32[]{:S(2)}) async-start(), calls=%async_computation.20 | async-start | bytes 13271040
  479.8 0.7 copy-start.9
  479.8 131.8 %all-gather.16.cloned.1.call-start = ((), (), s32[]{:S(2)}) async-start(), calls=%async_computation.11 | async-start | bytes 13271040 | tf_op jit(solution)/shard_map/all_gather | solution.py:74
  593.2 87.2 %copy-start.2 = (f32[128,2048]{1,0:T(8,128)S(1)}, f32[128,2048]{1,0:T(8,128)}, u32[]{:S(2)}) copy-start(f32[128,2048]{1,0:T(8,128)} %get-tuple-element.18) | copy-start | bytes 3145732
  593.2 87.2 %all-gather.18.cloned.1.call-start = ((), (), s32[]{:S(2)}) async-start(), calls=%async_computation.12 | async-start | bytes 1474560 | tf_op jit(solution)/shard_map/all_gather | solution.py:35
  640.4 146.3 %reduce-scatter.33.cloned.1.call-start = ((), (), s32[]{:S(2)}) async-start(), calls=%async_computation.21 | async-start | bytes 1474560
  724.2 115.5 %reduce-scatter.35.cloned.1.call-start = ((), (), s32[]{:S(2)}) async-start(), calls=%async_computation.22 | async-start | bytes 13271040
  825.6 135.2 %all-gather.20.cloned.1.call-start = ((), (), s32[]{:S(2)}) async-start(), calls=%async_computation.13 | async-start | bytes 13271040 | tf_op jit(solution)/shard_map/all_gather | solution.py:74
  942.4 87.2 %copy-start.3 = (f32[128,2048]{1,0:T(8,128)S(1)}, f32[128,2048]{1,0:T(8,128)}, u32[]{:S(2)}) copy-start(f32[128,2048]{1,0:T(8,128)} %get-tuple-element.18) | copy-start | bytes 3145732
  942.4 87.2 %all-gather.22.cloned.1.call-start = ((), (), s32[]{:S(2)}) async-start(), calls=%async_computation.14 | async-start | bytes 1474560 | tf_op jit(solution)/shard_map/all_gather | solution.py:35
  989.7 146.4 %reduce-scatter.37.cloned.1.call-start = ((), (), s32[]{:S(2)}) async-start(), calls=%async_computation.23 | async-start | bytes 1474560
  1073.5 115.5 %reduce-scatter.39.cloned.1.call-start = ((), (), s32[]{:S(2)}) async-start(), calls=%async_computation.24 | async-start | bytes 13271040
  1175.0 94.1 %all-gather.24.cloned.1.call-start = ((), (), s32[]{:S(2)}) async-start(), calls=%async_computation.15 | async-start | bytes 13271040 | tf_op jit(solution)/shard_map/all_gather | solution.py:74
  1250.6 87.2 %copy-start.4 = (f32[128,2048]{1,0:T(8,128)S(1)}, f32[128,2048]{1,0:T(8,128)}, u32[]{:S(2)}) copy-start(f32[128,2048]{1,0:T(8,128)} %get-tuple-element.18) | copy-start | bytes 3145732
  1250.6 87.2 %copy-start.6 = (s32[2048]{0:T(1024)S(1)}, s32[2048]{0:T(1024)}, u32[]{:S(2)}) copy-start(s32[2048]{0:T(1024)} %copy-done.5) | copy-start | bytes 24580
  1250.6 87.2 %copy-start.8 = (s32[128]{0:T(128)S(1)}, s32[128]{0:T(128)}, u32[]{:S(2)}) copy-start(s32[128]{0:T(128)} %param.12) | copy-start | bytes 1540
  1250.7 87.2 %all-gather.26.cloned.1.call-start = ((), (), s32[]{:S(2)}) async-start(), calls=%async_computation.16 | async-start | bytes 1474560 | tf_op jit(solution)/shard_map/all_gather | solution.py:35
Sparse Core Ops, SparseCore 0:
  37.2 39.8 all-gather.9
  120.5 62.3 reduce-scatter.24
  221.9 13.9 reduce-scatter.26
  243.2 22.2 all-gather.11
  294.5 39.7 all-gather.13
  378.4 62.3 reduce-scatter.28
  479.9 13.8 reduce-scatter.30
  593.3 18.2 all-gather.15
  640.5 39.7 all-gather.17
  724.3 62.2 reduce-scatter.32
  825.7 13.9 reduce-scatter.34
  942.6 18.2 all-gather.19
  989.8 39.7 all-gather.21
  1073.7 62.3 reduce-scatter.36
  1175.1 13.9 reduce-scatter.38
  1250.8 18.2 all-gather.23
  1298.0 39.7 all-gather.25
